TPU v7x, 32 devices: a whole 2x2x4 slice. The times are simulated.
32 devices in a mesh: grp: 2 (over x), scan: 8 (over z, y), det: 2 (over core).
Axes of the slice: x: 2, y: 2, z: 4, core: 2. Of those that a mesh axis runs over, the one named last changes fastest.
Arguments:
- spectra: float32 [16384, 4096], P(('grp', 'scan'), 'det'), parts along dimension 0, may hold values from 0 to 544, as said below
- basis: float32 [64, 4096], P('grp', 'det'), parts along dimension 0, may hold values from 0.03 to 8, as said below
- loadings: float32 [64, 8192], P('grp', 'scan'), parts along dimension 0, may hold values from 0.005 to 6, as said below
Outputs:
- new_loadings: float32 [64, 8192], P('grp', 'scan'), parts along dimension 0
- new_basis: float32 [64, 4096], P('grp', 'det'), parts along dimension 0
There are 2 independent parts, one for each index of `grp`. A program takes and returns all parts, laid end to end along the dimension named above; each array names one. Nothing has to cross between parts.
Inputs may be any that keep to these rules, and one draw needn't show every extreme that they name: `spectra`: intensities are nonnegative. `basis`: entries are positive. `loadings`: entries are positive.
All inputs are finite; a program needn't handle non-finite values.
Results may differ from a plain program's by a relative error of at most 0.00005.
Values sent between devices are 32-bit elements; how exact they have to be, the bound alone decides.
A program may use at most 64 MiB of HBM per device.

v0:
```python
import jax
import jax.numpy as jnp
from jax import lax
from jax.sharding import PartitionSpec as P

HIGHEST = lax.Precision.HIGHEST


def swapped(block, axis, stride):
    count = lax.axis_size(axis)
    route = []
    for low in range(count):
        high = low | 1 << stride
        if high != low and high < count:
            route += [(low, high), (high, low)]
    return lax.ppermute(block, axis, route)


def per_device(spectra, basis, loadings):
    partner = swapped(basis, "det", 0)
    tied = 0.5 * (basis + jnp.flip(partner, 1))
    local_numer = lax.dot_general(tied, spectra, (((1,), (1,)), ((), ())), precision=HIGHEST)
    gram = 2.0 * lax.dot_general(tied, tied, (((1,), (1,)), ((), ())), precision=HIGHEST)
    numer_h = lax.psum(local_numer, "det")
    new_loadings = loadings * numer_h / jnp.dot(gram, loadings, precision=HIGHEST)
    w_terms = jnp.dot(new_loadings, spectra, precision=HIGHEST)
    cross_terms = lax.dot_general(
        new_loadings, new_loadings, (((1,), (1,)), ((), ())), precision=HIGHEST
    )
    numer_w, cross = lax.psum((w_terms, cross_terms), "scan")
    mirrored = swapped(numer_w, "det", 0)
    tied_numer = 0.5 * (numer_w + jnp.flip(mirrored, 1))
    new_basis = tied * tied_numer / jnp.dot(cross, tied, precision=HIGHEST)
    return (new_loadings, new_basis)


def solution(mesh):
    in_specs = (P(("grp", "scan"), "det"), P("grp", "det"), P("grp", "scan"))
    out_specs = (P("grp", "scan"), P("grp", "det"))
    return jax.shard_map(
        per_device, mesh=mesh, in_specs=in_specs, out_specs=out_specs, check_vma=False
    )
```

profile of v0, /device:TPU:0, one launch (start us, length us, event | category | flops | bytes accessed | tf_op | source)
XLA Modules:
  0.0 169.7 jit_solution(7217789478776410331)
XLA Ops:
  7.2 0.0 copy-start.1
  7.2 0.0 all-reduce.3.cloned.1.call-start
  7.2 0.6 collective-permute-start
  7.8 1.4 collective-permute-done
  9.2 1.2 rev.7
  10.3 1.0 add_multiply_fusion
  11.3 10.6 %fusion = f32[32,1024]{1,0:T(8,128)} fusion(f32[32,2048]{1,0:T(8,128)S(1)} %add_multiply_fusion, f32[1024,2048]{1,0:T(8,128)} %param.3), kind=kOutput, calls=%fused_computation.4 | convolution fusion | flops 805306368 | bytes 8781824 | tf_op jit(solution)/shard_map/dot_general | solution.py:22
  21.9 0.0 all-reduce.3.cloned.1.call-update
  21.9 0.0 all-reduce.5.cloned.1.call-start
  22.0 0.3 convolution_multiply_fusion
  22.3 20.3 %all-reduce.3.cloned.1.call-done = f32[32,1024]{1,0:T(8,128)} async-done(((f32[32,1024]{1,0:T(8,128)}), f32[32,1024]{1,0:T(8,128)}) %all-reduce.3.cloned.1.call-update) | async-done | bytes 131088 | tf_op jit(solution)/shard_map/psum | solution.py:24
  42.6 0.0 copy-done.1
  42.6 1.2 convolution_divide_fusion
  43.8 0.0 copy-start
  43.8 7.9 %fusion.1 = f32[32,2048]{1,0:T(8,128)} fusion(f32[32,1024]{1,0:T(8,128)S(1)} %convolution_divide_fusion, f32[1024,2048]{1,0:T(8,128)} %param.3), kind=kOutput, calls=%fused_computation.5 | convolution fusion | flops 805306368 | bytes 8781824 | tf_op jit(solution)/shard_map/dot_general | solution.py:26
  51.7 0.0 all-reduce.5.cloned.1.call-update
  51.7 72.4 %all-reduce.5.cloned.1.call-done = f32[32,2048]{1,0:T(8,128)} async-done(((f32[32,2048]{1,0:T(8,128)}), f32[32,2048]{1,0:T(8,128)}) %all-reduce.5.cloned.1.call-update) | async-done | bytes 262160 | tf_op jit(solution)/shard_map/psum | solution.py:30
  124.1 0.0 collective-permute-start.1
  124.1 0.2 fusion.2
  124.3 35.3 %psum.23 = f32[32,32]{1,0:T(8,128)S(1)} all-reduce(f32[32,32]{1,0:T(8,128)S(1)} %fusion.2), channel_id=1, replica_groups=mesh['grp'=2,'scan'=8,'det'=2] {'scan'}, use_global_device_ids=true, to_apply=%region_2.3 | all-reduce | flops 1024 | bytes 8192 | tf_op jit(solution)/shard_map/psum | solution.py:30
  159.7 0.0 collective-permute-done.1
  159.7 1.2 rev.8
  160.8 2.0 %multiply_divide_fusion = f32[32,2048]{1,0:T(8,128)} fusion(f32[32,2048]{1,0:T(8,128)S(1)} %add_multiply_fusion, f32[32,2048]{1,0:T(8,128)} %all-reduce.5.cloned.1.call-done, f32[32,2048]{1,0:T(8,128)S(1)} %rev.8, f32[32,32]{1,0:T(8,128)S(1)} %psum.23), kind=kOutput, calls=%fused_computation.2 | convolution fusion | flops 25427968 | bytes 1052672 | tf_op jit(solution)/shard_map/dot_general | solution.py:33
  162.9 0.0 copy-done
Async XLA Ops:
  7.2 35.4 %copy-start.1 = (f32[32,1024]{1,0:T(8,128)S(1)}, f32[32,1024]{1,0:T(8,128)}, u32[]{:S(2)}) copy-start(f32[32,1024]{1,0:T(8,128)} %param.5) | copy-start | bytes 393220
  7.2 35.4 %all-reduce.3.cloned.1.call-start = ((), (), s32[]{:S(2)}) async-start(), calls=%async_computation | async-start | bytes 262144 | tf_op jit(solution)/shard_map/psum | solution.py:24
  7.2 1.9 %collective-permute-start = (f32[32,2048]{1,0:T(8,128)}, f32[32,2048]{1,0:T(8,128)S(1)}, u32[]{:S(2)}, u32[]{:S(2)}) collective-permute-start(f32[32,2048]{1,0:T(8,128)} %param.4), channel_id=1, source_target_pairs={{0,1},{1,0},{2,3},{3,2},{4,5},{5,4},{6,7},{7,6},{8,9},{9,8},{10,11... | collective-permute-start | bytes 786440 | tf_op jit(solution)/shard_map/ppermute | solution.py:16
  21.9 102.2 %all-reduce.5.cloned.1.call-start = ((), (), s32[]{:S(2)}) async-start(), calls=%async_computation.1 | async-start | bytes 524288 | tf_op jit(solution)/shard_map/psum | solution.py:30
  43.8 119.1 %copy-start = (f32[32,1024]{1,0:T(8,128)}, f32[32,1024]{1,0:T(8,128)S(1)}, u32[]{:S(2)}) copy-start(f32[32,1024]{1,0:T(8,128)S(1)} %convolution_divide_fusion) | copy-start | bytes 393220
  124.1 35.6 %collective-permute-start.1 = (f32[32,2048]{1,0:T(8,128)}, f32[32,2048]{1,0:T(8,128)S(1)}, u32[]{:S(2)}, u32[]{:S(2)}) collective-permute-start(f32[32,2048]{1,0:T(8,128)} %all-reduce.5.cloned.1.call-done), channel_id=1, source_target_pairs={{0,1},{1,0},{2,3},{3,2},{4,5},{5,4},{6,7},{7,6},{8,9},{9,8},{10,11... | collective-permute-start | bytes 786440 | tf_op jit(solution)/shard_map/ppermute | solution.py:16
Sparse Core Ops, SparseCore 0:
  22.0 20.5 all-reduce.2
  51.8 72.1 all-reduce.4
where the time goes:
time: 170 us
  waiting for transfers between devices  94 us (55%)
  blocking collectives  35.3 us (21%)
  matrix products  22.3 us (13%)
  between operations  14.1 us (8%)
  local copies, waits for them, and re-layouts  2.34 us (1%)
    psum x1, waiting for transfers between devices, per_device(): numer_w, cross = lax.psum((w_terms, cross_terms), 'scan')  72.4 us
    psum x1, blocking collectives, per_device(): numer_w, cross = lax.psum((w_terms, cross_terms), 'scan')  35.3 us
    psum x1, waiting for transfers between devices, per_device(): numer_h = lax.psum(local_numer, 'det')  20.3 us
    dot_general x1, matrix products, per_device(): lax.dot_general(tied, spectra, (((1,), (1,)), ((), ())), precision=HIGHEST)  10.6 us
    dot_general x1, matrix products, per_device(): w_terms = jnp.dot(new_loadings, spectra, precision=HIGHEST)  7.91 us
  transfers between devices with their start and end apart: 4, of which 3 were waited for; matrix products, arithmetic and copies ran while one was open for 0% of the time, Pallas kernels for 0%

commit v1 on v0

--- a/solution.py
+++ b/solution.py
@@ -21,7 +21,7 @@
     tied = 0.5 * (basis + jnp.flip(partner, 1))
     local_numer = lax.dot_general(tied, spectra, (((1,), (1,)), ((), ())), precision=HIGHEST)
     gram = 2.0 * lax.dot_general(tied, tied, (((1,), (1,)), ((), ())), precision=HIGHEST)
-    numer_h = lax.psum(local_numer, "det")
+    numer_h = jnp.sum(lax.all_gather(local_numer, "det"), axis=0)
     new_loadings = loadings * numer_h / jnp.dot(gram, loadings, precision=HIGHEST)
     w_terms = jnp.dot(new_loadings, spectra, precision=HIGHEST)
     cross_terms = lax.dot_general(

time: 170 us -> 152 us (0.89)
  waiting for transfers between devices: 94 us -> 75.1 us
  blocking collectives: 35.3 us -> 37.3 us
    psum x1 -> x0, waiting for transfers between devices: 20.3 us -> none  [per_device(): numer_h = lax.psum(local_numer, 'det')]
    all_gather x0 -> x1, blocking collectives: none -> 2 us  [per_device(): numer_h = jnp.sum(lax.all_gather(local_numer, 'det'), axis=0)]
  transfers between devices with their start and end apart: 4 -> 3, of which waited for: 3 -> 2; matrix products, arithmetic and copies ran while one was open for 0% -> 0% of each run, Pallas kernels for 0% -> 0%
where the time goes in v1:
time: 152 us; the launch traced here: 151 us
  waiting for transfers between devices  75.1 us (49%)
  blocking collectives  37.3 us (25%)
  matrix products  20.8 us (14%)
  between operations  14.1 us (9%)
  local copies, waits for them, and re-layouts  2.34 us (2%)
    psum x1, waiting for transfers between devices, per_device(): numer_w, cross = lax.psum((w_terms, cross_terms), 'scan')  73.7 us
    psum x1, blocking collectives, per_device(): numer_w, cross = lax.psum((w_terms, cross_terms), 'scan')  35.3 us
    dot_general x1, matrix products, per_device(): lax.dot_general(tied, spectra, (((1,), (1,)), ((), ())), precision=HIGHEST)  9.97 us
    dot_general x1, matrix products, per_device(): w_terms = jnp.dot(new_loadings, spectra, precision=HIGHEST)  7.91 us
  transfers between devices with their start and end apart: 3, of which 2 were waited for; matrix products, arithmetic and copies ran while one was open for 0% of the time, Pallas kernels for 0%

profile of v1, /device:TPU:0, one launch (start us, length us, event | category | flops | bytes accessed | tf_op | source)
XLA Modules:
  0.0 151.3 jit_solution(17699069668944774600)
XLA Ops:
  7.2 0.0 copy-start.1
  7.2 0.0 all-reduce.2.cloned.1.call-start
  7.2 0.6 collective-permute-start
  7.8 1.4 collective-permute-done
  9.2 1.2 rev.7
  10.3 1.0 add_multiply_fusion
  11.3 0.4 convolution_multiply_fusion
  11.7 10.0 %fusion = f32[32,1024]{1,0:T(8,128)S(1)} fusion(f32[32,2048]{1,0:T(8,128)S(1)} %add_multiply_fusion, f32[1024,2048]{1,0:T(8,128)} %param.3), kind=kOutput, calls=%fused_computation.4 | convolution fusion | flops 805306368 | bytes 8781824 | tf_op jit(solution)/shard_map/dot_general | solution.py:22
  21.7 2.0 %all-gather = f32[64,1024]{1,0:T(8,128)S(1)} all-gather(f32[32,1024]{1,0:T(8,128)S(1)} %fusion), channel_id=2, replica_groups=mesh['grp'=2,'scan'=8,'det'=2] {'det'}, dimensions={0}, use_global_device_ids=true | all-gather | bytes 393216 | tf_op jit(solution)/shard_map/all_gather | solution.py:24
  23.7 0.0 copy-done.1
  23.7 0.3 convolution_divide_fusion
  24.0 0.0 copy-start
  24.0 7.9 %fusion.1 = f32[32,2048]{1,0:T(8,128)} fusion(f32[32,1024]{1,0:T(8,128)S(1)} %convolution_divide_fusion, f32[1024,2048]{1,0:T(8,128)} %param.3), kind=kOutput, calls=%fused_computation.5 | convolution fusion | flops 805306368 | bytes 8781824 | tf_op jit(solution)/shard_map/dot_general | solution.py:26
  31.9 0.0 all-reduce.2.cloned.1.call-update
  31.9 73.7 %all-reduce.2.cloned.1.call-done = f32[32,2048]{1,0:T(8,128)} async-done(((f32[32,2048]{1,0:T(8,128)}), f32[32,2048]{1,0:T(8,128)}) %all-reduce.2.cloned.1.call-update) | async-done | bytes 262160 | tf_op jit(solution)/shard_map/psum | solution.py:30
  105.7 0.0 collective-permute-start.1
  105.7 0.2 fusion.2
  105.9 35.3 %psum.15 = f32[32,32]{1,0:T(8,128)S(1)} all-reduce(f32[32,32]{1,0:T(8,128)S(1)} %fusion.2), channel_id=1, replica_groups=mesh['grp'=2,'scan'=8,'det'=2] {'scan'}, use_global_device_ids=true, to_apply=%region_2.3 | all-reduce | flops 1024 | bytes 8192 | tf_op jit(solution)/shard_map/psum | solution.py:30
  141.2 0.0 collective-permute-done.1
  141.2 1.2 rev.8
  142.4 2.0 %multiply_divide_fusion = f32[32,2048]{1,0:T(8,128)} fusion(f32[32,2048]{1,0:T(8,128)S(1)} %add_multiply_fusion, f32[32,2048]{1,0:T(8,128)} %all-reduce.2.cloned.1.call-done, f32[32,2048]{1,0:T(8,128)S(1)} %rev.8, f32[32,32]{1,0:T(8,128)S(1)} %psum.15), kind=kOutput, calls=%fused_computation.2 | convolution fusion | flops 25427968 | bytes 1052672 | tf_op jit(solution)/shard_map/dot_general | solution.py:33
  144.4 0.0 copy-done
  (1 shorter events, 0.0 us)
Async XLA Ops:
  7.2 16.5 %copy-start.1 = (f32[32,1024]{1,0:T(8,128)S(1)}, f32[32,1024]{1,0:T(8,128)}, u32[]{:S(2)}) copy-start(f32[32,1024]{1,0:T(8,128)} %param.5) | copy-start | bytes 393220
  7.2 98.5 %all-reduce.2.cloned.1.call-start = ((), (), s32[]{:S(2)}) async-start(), calls=%async_computation | async-start | bytes 524288 | tf_op jit(solution)/shard_map/psum | solution.py:30
  7.2 1.9 %collective-permute-start = (f32[32,2048]{1,0:T(8,128)}, f32[32,2048]{1,0:T(8,128)S(1)}, u32[]{:S(2)}, u32[]{:S(2)}) collective-permute-start(f32[32,2048]{1,0:T(8,128)} %param.4), channel_id=1, source_target_pairs={{0,1},{1,0},{2,3},{3,2},{4,5},{5,4},{6,7},{7,6},{8,9},{9,8},{10,11... | collective-permute-start | bytes 786440 | tf_op jit(solution)/shard_map/ppermute | solution.py:16
  24.0 120.5 %copy-start = (f32[32,1024]{1,0:T(8,128)}, f32[32,1024]{1,0:T(8,128)S(1)}, u32[]{:S(2)}) copy-start(f32[32,1024]{1,0:T(8,128)S(1)} %convolution_divide_fusion) | copy-start | bytes 393220
  105.7 35.6 %collective-permute-start.1 = (f32[32,2048]{1,0:T(8,128)}, f32[32,2048]{1,0:T(8,128)S(1)}, u32[]{:S(2)}, u32[]{:S(2)}) collective-permute-start(f32[32,2048]{1,0:T(8,128)} %all-reduce.2.cloned.1.call-done), channel_id=1, source_target_pairs={{0,1},{1,0},{2,3},{3,2},{4,5},{5,4},{6,7},{7,6},{8,9},{9,8},{10,11... | collective-permute-start | bytes 786440 | tf_op jit(solution)/shard_map/ppermute | solution.py:16
Sparse Core Ops, SparseCore 0:
  32.0 73.5 all-reduce.1
